TPU v7x, 128 devices: a whole 4x4x4 slice. The times are simulated.
128 devices in a mesh: freq: 8 (over x, y_lo), tm: 16 (over z, y_hi, core).
Axes of the slice: x: 4, y: 4 (y_hi: 2, y_lo: 2; y = y_hi * 2 + y_lo), z: 4, core: 2. Of those that a mesh axis runs over, the one named last changes fastest.
Arguments:
- voltages: bfloat16 [2048, 530432], P(('tm', 'freq')), may hold values from -128 to 127, as said below
- fir_taps: float32 [4, 2048], replicated, may hold values from -3 to 3
Outputs:
- coherence: bfloat16 [2, 64, 2048, 2048], P(None, 'freq', 'tm')
Inputs may be any that keep to these rules, and one draw needn't show every extreme that they name: `voltages`: every sample is a whole number.
All inputs are finite; a program needn't handle non-finite values.
Results may differ from a plain program's by a relative error of at most 0.0073.
Values may be sent and summed in bfloat16 or wider, within the bound.
A program may use at most 192 MiB of HBM per device.

v0:
```python
import math
import jax
import jax.numpy as jnp
from jax import lax
from jax.sharding import PartitionSpec as P

P_SIZE = 2048
TAPS = 4
FIRST_BIN = 512
CH_DEV = 8
S = 256


def dft_table(channels):
    points = jnp.arange(P_SIZE, dtype=jnp.int32)
    bins = FIRST_BIN + jnp.arange(channels, dtype=jnp.int32)
    phase = points[:, None] * bins[None, :] % P_SIZE
    angle = 2.0 * math.pi / P_SIZE * phase.astype(jnp.float32)
    twiddle = jnp.stack([jnp.cos(angle), -jnp.sin(angle)], axis=2)
    return twiddle.reshape(P_SIZE, 2 * channels).astype(jnp.bfloat16)


def filter_frames(block, fir_taps):
    inputs_here = block.shape[0]
    samples = block.astype(jnp.float32).reshape(inputs_here, S + TAPS - 1, P_SIZE)
    frames = fir_taps[0] * samples[:, 0:S]
    for tap_index in range(1, TAPS):
        frames = frames + fir_taps[tap_index] * samples[:, tap_index : tap_index + S]
    return frames.astype(jnp.bfloat16).reshape(inputs_here * S, P_SIZE)


def correlate(own_spectra, column_block):
    slab = own_spectra.shape[0]
    rows_here = own_spectra.shape[2]
    width = column_block.shape[2]
    left_rows = own_spectra.reshape(slab, 2 * rows_here, S)
    right_rows = column_block.reshape(slab, 2 * width, S)
    products = lax.dot_general(
        left_rows, right_rows, (((2,), (2,)), ((0,), (0,))), preferred_element_type=jnp.float32
    )
    products = products.reshape(slab, 2, rows_here, 2, width)
    real_part = products[:, 0, :, 0] + products[:, 1, :, 1]
    imag_part = products[:, 1, :, 0] - products[:, 0, :, 1]
    return jnp.stack([real_part, imag_part])


def on_device(voltages, fir_taps):
    freq_count = lax.axis_size("freq")
    channels = CH_DEV * freq_count
    inputs_here = voltages.shape[0]
    frames = filter_frames(voltages, fir_taps)
    twiddle = dft_table(channels)
    spectra = lax.dot_general(
        twiddle, frames, (((0,), (1,)), ((), ())), preferred_element_type=jnp.float32
    )
    spectra = spectra.astype(jnp.bfloat16).reshape(channels, 2, inputs_here, S)
    own_spectra = lax.all_to_all(spectra, "freq", split_axis=0, concat_axis=2, tiled=True)
    all_spectra = lax.all_gather(own_spectra, "tm", axis=2, tiled=True)
    raw_sums = correlate(own_spectra, all_spectra)
    wide = own_spectra.astype(jnp.float32)
    powers = jnp.sum(wide * wide, axis=(1, 3)) / S + 1e-06
    powers_all = lax.all_gather(powers, "tm", axis=1, tiled=True)
    row_scale = lax.rsqrt(powers) / S
    column_scale = lax.rsqrt(powers_all)
    coherence = raw_sums * row_scale[None, :, :, None] * column_scale[None, :, None, :]
    return coherence.astype(jnp.bfloat16)


def solution(mesh):
    placed = (P(("tm", "freq"), None), P())
    return jax.shard_map(
        on_device,
        mesh=mesh,
        in_specs=placed,
        out_specs=P(None, "freq", "tm", None),
        check_vma=False,
    )
```

profile of v0, /device:TPU:1, one launch (start us, length us, event | category | flops | bytes accessed | tf_op | source)
XLA Modules:
  0.0 373.9 jit_solution(2463869961442593070)
XLA Ops:
  6.5 0.0 all-gather.2.cloned.1.call-start
  6.5 0.9 fusion.15
  7.5 2.5 cosine_convert_fusion
  9.9 0.1 pad_maximum_fusion
  10.0 0.5 copy.13
  10.5 0.2 convert_element_type.41
  10.8 25.4 %reshape.197 = f32[16,259,2048]{2,1,0:T(8,128)} reshape(bf16[16,530432]{1,0:T(8,128)(2,1)} %param.2) | data formatting | bytes 50921472 | tf_op jit(solution)/shard_map/reshape | solution.py:25
  36.1 49.4 %fusion.1 = bf16[16,256,2048]{2,1,0:T(8,128)(2,1)} fusion(f32[16,259,2048]{2,1,0:T(8,128)} %reshape.197, f32[2048]{0:T(1024)S(1)} %bitcast.36, f32[2048]{0:T(1024)S(1)} %bitcast.37, f32[2048]{0:T(1024)S(1)} %bitcast.35, f32[2048]{0:T(1024)S(1)} %bitcast.34), kind=kLoop, calls=%fused_computation.2 | loop fusion | flops 67108864 | bytes 151027712 | tf_op jit(solution)/shard_map/convert_element_type | solution.py:29
  85.5 11.4 %convolution_convert_fusion = bf16[128,4096]{1,0:T(8,128)(2,1)S(1)} fusion(bf16[2048,128]{0,1:T(8,128)(2,1)S(1)} %convert_element_type.41, bf16[4096,2048]{1,0:T(8,128)(2,1)} %bitcast.26), kind=kOutput, calls=%fused_computation.15 | convolution fusion | flops 2148007936 | bytes 18350080 | tf_op jit(solution)/shard_map/dot_general | solution.py:53
  96.9 0.2 copy.23
  97.2 20.0 %all_to_all.18 = bf16[64,2,16,256]{3,2,1,0:T(8,128)(2,1)S(1)} all-to-all(bf16[64,2,16,256]{3,2,1,0:T(8,128)(2,1)S(1)} %bitcast.33), channel_id=1, replica_groups=mesh['freq'=8,'tm'=16] {'freq'}, dimensions={0} | all-to-all | bytes 2097152 | tf_op jit(solution)/shard_map/all_to_all | solution.py:57
  117.1 1.1 copy.14
  118.2 0.0 all-gather.2.cloned.1.call-update
  118.3 0.3 multiply_reduce_fusion
  118.5 0.1 add.76
  118.6 27.9 %all_gather.7 = f32[8,2048]{1,0:T(8,128)S(1)} all-gather(f32[8,128]{1,0:T(8,128)S(1)} %add.76), channel_id=1, replica_groups=mesh['freq'=8,'tm'=16] {'tm'}, dimensions={1}, use_global_device_ids=true | all-gather | bytes 69632 | tf_op jit(solution)/shard_map/all_gather | solution.py:62
  146.5 83.9 %all-gather.2.cloned.1.call-done = bf16[8,2,2048,256]{3,2,1,0:T(8,128)(2,1)} async-done(((bf16[8,2,128,256]{3,2,1,0:T(8,128)(2,1)}), bf16[8,2,2048,256]{3,2,1,0:T(8,128)(2,1)}) %all-gather.2.cloned.1.call-update) | async-done | bytes 16777232 | tf_op jit(solution)/shard_map/all_gather | solution.py:58
  230.5 17.4 %fusion.16 = f32[8,256,4096]{2,1,0:T(8,128)} fusion(bf16[8,256,256]{2,1,0:T(8,128)(2,1)} %bitcast.29, bf16[8,4096,256]{2,1,0:T(8,128)(2,1)} %bitcast.27), kind=kOutput, calls=%fused_computation.34 | convolution fusion | flops 4294967296 | bytes 51380224 | tf_op jit(solution)/shard_map/dot_general | solution.py:38
  247.9 42.6 %reshape.195 = f32[8,2,128,2,2048]{4,3,2,1,0:T(2,128)} reshape(f32[8,256,4096]{2,1,0:T(8,128)} %fusion.16) | data formatting | bytes 67108864 | tf_op jit(solution)/shard_map/reshape | solution.py:41
  290.6 39.8 %fusion.14 = (f32[8,1,128,1,2048]{4,3,2,1,0:T(1,128)}, f32[8,1,128,1,2048]{4,3,2,1,0:T(1,128)}, f32[8,1,128,1,2048]{4,3,2,1,0:T(1,128)}, f32[8,1,128,1,2048]{4,3,2,1,0:T(1,128)}) fusion(f32[8,2,128,2,2048]{4,3,2,1,0:T(2,128)} %reshape.195), kind=kLoop, calls=%fused_computation.32 | loop fusion | bytes 67108864 | tf_op jit(solution)/shard_map/slice | solution.py:42
  330.4 26.8 %fusion.6 = (f32[1,8,128,2048]{3,2,1,0:T(8,128)}, f32[1,8,128,2048]{3,2,1,0:T(8,128)}) fusion(f32[8,1,128,1,2048]{4,3,2,1,0:T(1,128)} %get-tuple-element.8, f32[8,1,128,1,2048]{4,3,2,1,0:T(1,128)} %get-tuple-element.6, f32[8,1,128,1,2048]{4,3,2,1,0:T(1,128)} %get-tuple-element.7, f32[8,1,128,1,2048]{4,3,2,1,0:T(1,128)} %get-tuple-element.5), kind=kLoop, calls=%fused_computation.12 | loop fusion | flops 4194304 | bytes 50331648 | tf_op jit(solution)/shard_map/sub | solution.py:43
  357.2 9.9 %fusion.5 = bf16[2,8,128,2048]{3,2,1,0:T(8,128)(2,1)} fusion(f32[1,8,128,2048]{3,2,1,0:T(8,128)} %get-tuple-element.15, f32[1,8,128,2048]{3,2,1,0:T(8,128)} %get-tuple-element.16, f32[8,2048]{1,0:T(8,128)S(1)} %rsqrt.11, f32[8,128]{1,0:T(8,128)S(1)} %rsqrt_multiply_fusion), kind=kLoop, calls=%fused_computation.10 | loop fusion | flops 16777216 | bytes 25235456 | tf_op jit(solution)/shard_map/convert_element_type | solution.py:66
  (4 shorter events, 0.0 us)
Async XLA Ops:
  6.5 224.0 %all-gather.2.cloned.1.call-start = ((), (), s32[]{:S(2)}) async-start(), calls=%async_computation.1 | async-start | bytes 17825792 | tf_op jit(solution)/shard_map/all_gather | solution.py:58
Sparse Core Ops, SparseCore 0:
  118.4 112.0 all-gather.1
where the time goes:
time: 375 us; the launch traced here: 374 us
  local copies, waits for them, and re-layouts  111 us (30%)
  other arithmetic  88.9 us (24%)
  waiting for transfers between devices  84 us (22%)
  blocking collectives  47.9 us (13%)
  matrix products  28.8 us (8%)
  between operations  13.5 us (4%)
    all_gather x1, waiting for transfers between devices, on_device(): all_spectra = lax.all_gather(own_spectra, 'tm', axis=2, tiled=True)  83.9 us
    convert_element_type x1, other arithmetic, filter_frames(): return frames.astype(jnp.bfloat16).reshape(inputs_here * S, P_SIZE)  49.4 us
    reshape x1, local copies, waits for them, and re-layouts, correlate(): products = products.reshape(slab, 2, rows_here, 2, width)  42.6 us
    slice x1, local copies, waits for them, and re-layouts, correlate(): real_part = products[:, 0, :, 0] + products[:, 1, :, 1]  39.8 us
    all_gather x1, blocking collectives, on_device(): powers_all = lax.all_gather(powers, 'tm', axis=1, tiled=True)  27.9 us
    sub x1, other arithmetic, correlate(): imag_part = products[:, 1, :, 0] - products[:, 0, :, 1]  26.8 us
    reshape x1, local copies, waits for them, and re-layouts, filter_frames(): block.astype(jnp.float32).reshape(inputs_here, S + TAPS - 1, P_SIZE)  25.4 us
    all_to_all x1, blocking collectives, on_device(): lax.all_to_all(spectra, 'freq', split_axis=0, concat_axis=2, tiled=True)  20 us
  transfers between devices with their start and end apart: 1, of which 1 were waited for; matrix products, arithmetic and copies ran while one was open for 0% of the time, Pallas kernels for 0%

commit v1 on v0

--- a/solution.py
+++ b/solution.py
@@ -54,7 +54,9 @@
         twiddle, frames, (((0,), (1,)), ((), ())), preferred_element_type=jnp.float32
     )
     spectra = spectra.astype(jnp.bfloat16).reshape(channels, 2, inputs_here, S)
-    own_spectra = lax.all_to_all(spectra, "freq", split_axis=0, concat_axis=2, tiled=True)
+    pieces = jnp.split(spectra, lax.axis_size("freq"), axis=0)
+    received = lax.all_to_all(jnp.stack(pieces), "freq", 0, 0)
+    own_spectra = jnp.concatenate(received, axis=2)
     all_spectra = lax.all_gather(own_spectra, "tm", axis=2, tiled=True)
     raw_sums = correlate(own_spectra, all_spectra)
     wide = own_spectra.astype(jnp.float32)

time: 375 us -> 375 us (level)
  no operation moved by 1% of the time
where the time goes in v1:
time: 375 us; the launch traced here: 374 us
  local copies, waits for them, and re-layouts  111 us (30%)
  other arithmetic  88.9 us (24%)
  waiting for transfers between devices  84 us (22%)
  blocking collectives  47.7 us (13%)
  matrix products  28.8 us (8%)
  between operations  13.6 us (4%)
    all_gather x1, waiting for transfers between devices, on_device(): all_spectra = lax.all_gather(own_spectra, 'tm', axis=2, tiled=True)  84 us
    convert_element_type x1, other arithmetic, filter_frames(): return frames.astype(jnp.bfloat16).reshape(inputs_here * S, P_SIZE)  49.4 us
    reshape x1, local copies, waits for them, and re-layouts, correlate(): products = products.reshape(slab, 2, rows_here, 2, width)  42.6 us
    slice x1, local copies, waits for them, and re-layouts, correlate(): real_part = products[:, 0, :, 0] + products[:, 1, :, 1]  39.8 us
    all_gather x1, blocking collectives, on_device(): powers_all = lax.all_gather(powers, 'tm', axis=1, tiled=True)  27.7 us
    sub x1, other arithmetic, correlate(): imag_part = products[:, 1, :, 0] - products[:, 0, :, 1]  26.8 us
    reshape x1, local copies, waits for them, and re-layouts, filter_frames(): block.astype(jnp.float32).reshape(inputs_here, S + TAPS - 1, P_SIZE)  25.3 us
    all_to_all x1, blocking collectives, on_device(): received = lax.all_to_all(jnp.stack(pieces), 'freq', 0, 0)  20 us
  transfers between devices with their start and end apart: 1, of which 1 were waited for; matrix products, arithmetic and copies ran while one was open for 0% of the time, Pallas kernels for 0%

profile of v1, /device:TPU:1, one launch (start us, length us, event | category | flops | bytes accessed | tf_op | source)
XLA Modules:
  0.0 374.0 jit_solution(15326560489870455154)
XLA Ops:
  6.5 0.0 all-gather.2.cloned.1.call-start
  6.5 0.9 fusion.16
  7.5 2.5 cosine_convert_fusion
  9.9 0.1 pad_maximum_fusion
  10.0 0.5 copy.25
  10.5 0.2 convert_element_type.41
  10.8 25.3 %reshape.213 = f32[16,259,2048]{2,1,0:T(8,128)} reshape(bf16[16,530432]{1,0:T(8,128)(2,1)} %param.2) | data formatting | bytes 50921472 | tf_op jit(solution)/shard_map/reshape | solution.py:25
  36.1 49.4 %fusion.1 = bf16[16,256,2048]{2,1,0:T(8,128)(2,1)} fusion(f32[16,259,2048]{2,1,0:T(8,128)} %reshape.213, f32[2048]{0:T(1024)S(1)} %bitcast.68, f32[2048]{0:T(1024)S(1)} %bitcast.69, f32[2048]{0:T(1024)S(1)} %bitcast.67, f32[2048]{0:T(1024)S(1)} %bitcast.66), kind=kLoop, calls=%fused_computation.2 | loop fusion | flops 67108864 | bytes 151027712 | tf_op jit(solution)/shard_map/convert_element_type | solution.py:29
  85.5 11.4 %convolution_convert_fusion = bf16[128,4096]{1,0:T(8,128)(2,1)S(1)} fusion(bf16[2048,128]{0,1:T(8,128)(2,1)S(1)} %convert_element_type.41, bf16[4096,2048]{1,0:T(8,128)(2,1)} %bitcast.46), kind=kOutput, calls=%fused_computation.15 | convolution fusion | flops 2148007936 | bytes 18350080 | tf_op jit(solution)/shard_map/dot_general | solution.py:53
  96.9 0.1 fusion.15
  97.4 20.0 %all_to_all.5 = bf16[8,8,2,16,256]{4,3,2,1,0:T(8,128)(2,1)S(1)} all-to-all(bf16[8,8,2,16,256]{4,3,2,1,0:T(8,128)(2,1)S(1)} %constant_dynamic-update-slice_fusion), channel_id=1, replica_groups=mesh['freq'=8,'tm'=16] {'freq'}, dimensions={0} | all-to-all | bytes 2097152 | tf_op jit(solution)/shard_map/all_to_all | solution.py:58
  117.4 1.1 copy.26
  118.5 0.0 all-gather.2.cloned.1.call-update
  118.5 0.3 multiply_reduce_fusion
  118.8 0.1 add.76
  118.8 27.7 %all_gather.7 = f32[8,2048]{1,0:T(8,128)S(1)} all-gather(f32[8,128]{1,0:T(8,128)S(1)} %add.76), channel_id=1, replica_groups=mesh['freq'=8,'tm'=16] {'tm'}, dimensions={1}, use_global_device_ids=true | all-gather | bytes 69632 | tf_op jit(solution)/shard_map/all_gather | solution.py:64
  146.6 84.0 %all-gather.2.cloned.1.call-done = bf16[8,2,2048,256]{3,2,1,0:T(8,128)(2,1)} async-done(((bf16[8,2,128,256]{3,2,1,0:T(8,128)(2,1)}), bf16[8,2,2048,256]{3,2,1,0:T(8,128)(2,1)}) %all-gather.2.cloned.1.call-update) | async-done | bytes 16777232 | tf_op jit(solution)/shard_map/all_gather | solution.py:60
  230.6 17.4 %fusion.17 = f32[8,256,4096]{2,1,0:T(8,128)} fusion(bf16[8,256,256]{2,1,0:T(8,128)(2,1)} %bitcast.49, bf16[8,4096,256]{2,1,0:T(8,128)(2,1)} %bitcast.47), kind=kOutput, calls=%fused_computation.43 | convolution fusion | flops 4294967296 | bytes 51380224 | tf_op jit(solution)/shard_map/dot_general | solution.py:38
  248.0 42.6 %reshape.211 = f32[8,2,128,2,2048]{4,3,2,1,0:T(2,128)} reshape(f32[8,256,4096]{2,1,0:T(8,128)} %fusion.17) | data formatting | bytes 67108864 | tf_op jit(solution)/shard_map/reshape | solution.py:41
  290.6 39.8 %fusion.14 = (f32[8,1,128,1,2048]{4,3,2,1,0:T(1,128)}, f32[8,1,128,1,2048]{4,3,2,1,0:T(1,128)}, f32[8,1,128,1,2048]{4,3,2,1,0:T(1,128)}, f32[8,1,128,1,2048]{4,3,2,1,0:T(1,128)}) fusion(f32[8,2,128,2,2048]{4,3,2,1,0:T(2,128)} %reshape.211), kind=kLoop, calls=%fused_computation.40 | loop fusion | bytes 67108864 | tf_op jit(solution)/shard_map/slice | solution.py:42
  330.4 26.8 %fusion.6 = (f32[1,8,128,2048]{3,2,1,0:T(8,128)}, f32[1,8,128,2048]{3,2,1,0:T(8,128)}) fusion(f32[8,1,128,1,2048]{4,3,2,1,0:T(1,128)} %get-tuple-element.8, f32[8,1,128,1,2048]{4,3,2,1,0:T(1,128)} %get-tuple-element.6, f32[8,1,128,1,2048]{4,3,2,1,0:T(1,128)} %get-tuple-element.7, f32[8,1,128,1,2048]{4,3,2,1,0:T(1,128)} %get-tuple-element.5), kind=kLoop, calls=%fused_computation.12 | loop fusion | flops 4194304 | bytes 50331648 | tf_op jit(solution)/shard_map/sub | solution.py:43
  357.2 9.9 %fusion.5 = bf16[2,8,128,2048]{3,2,1,0:T(8,128)(2,1)} fusion(f32[1,8,128,2048]{3,2,1,0:T(8,128)} %get-tuple-element.23, f32[1,8,128,2048]{3,2,1,0:T(8,128)} %get-tuple-element.24, f32[8,2048]{1,0:T(8,128)S(1)} %rsqrt.11, f32[8,128]{1,0:T(8,128)S(1)} %rsqrt_multiply_fusion), kind=kLoop, calls=%fused_computation.10 | loop fusion | flops 16777216 | bytes 25235456 | tf_op jit(solution)/shard_map/convert_element_type | solution.py:68
  (20 shorter events, 0.3 us)
Async XLA Ops:
  6.5 224.0 %all-gather.2.cloned.1.call-start = ((), (), s32[]{:S(2)}) async-start(), calls=%async_computation.1 | async-start | bytes 17825792 | tf_op jit(solution)/shard_map/all_gather | solution.py:60
Sparse Core Ops, SparseCore 0:
  118.6 111.9 all-gather.1
